TPU v7x, 1024 devices: a whole 8x8x8 slice. The times are simulated.
1024 devices in a mesh: ctx: 256 (over z_hi, x, y, core), head: 4 (over z_lo).
Axes of the slice: x: 8, y: 8, z: 8 (z_hi: 2, z_lo: 4; z = z_hi * 4 + z_lo), core: 2. Of those that a mesh axis runs over, the one named last changes fastest.
Arguments:
- queries: bfloat16 [256, 256, 32, 128], P('ctx', 'head'), may hold values from -6 to 6
- keys: bfloat16 [256, 256, 4, 128], P('ctx', 'head'), may hold values from -6 to 6
- values: bfloat16 [256, 256, 4, 128], P('ctx', 'head'), may hold values from -6 to 6
Outputs:
- weighted: float32 [256, 256, 32, 128], P('ctx', None, 'head')
- row_max: float32 [32, 256, 256], P('head', 'ctx')
- row_sum: float32 [32, 256, 256], P('head', 'ctx')
All inputs are finite; a program needn't handle non-finite values.
Results may differ from a plain program's by a relative error of at most 0.0027.
Values may be sent and summed in bfloat16 or wider, within the bound.
A program may use at most 32 MiB of HBM per device.

v0:
```python
import math

import jax
import jax.numpy as jnp
from jax import lax
from jax.sharding import PartitionSpec as P

QUERY_HEADS = 32
KEY_VALUE_HEADS = 4
WIN = 8


def shifted(block, axis, distance):
    devices = range(lax.axis_size(axis))
    route = [((i - distance) % len(devices), i) for i in devices]
    return lax.ppermute(block, axis, route)


def positions(source, row_halves, period_length):
    row_ids = jnp.arange(2 * row_halves, dtype=jnp.int32)
    return jnp.where(
        row_ids < row_halves,
        2 * source * row_halves + row_ids,
        (2 * period_length - 1 - 2 * source) * row_halves + row_ids - row_halves,
    )


def local(queries, keys, values):
    query_all, key_all, value_all = (
        lax.all_to_all(queries, "head", split_axis=2, concat_axis=1, tiled=True),
        lax.all_to_all(keys, "head", split_axis=2, concat_axis=1, tiled=True),
        lax.all_to_all(values, "head", split_axis=2, concat_axis=1, tiled=True),
    )
    query_zig = query_all[0]
    key_zig = key_all[0]
    value_zig = value_all[0]
    row_halves = query_zig.shape[0] // 2
    period_length = lax.axis_size("ctx")
    own_index = lax.axis_index("ctx")
    key_list = [key_zig]
    value_list = [value_zig]
    current = (key_zig, value_zig)
    for stop_id in range(1, WIN):
        current = shifted((current[0], current[1]), "ctx", 1)
        key_list.append(current[0])
        value_list.append(current[1])
    key_row_block = jnp.concatenate(key_list, axis=0)
    value_row_block = jnp.concatenate(value_list, axis=0)
    sources = (own_index - jnp.arange(WIN, dtype=jnp.int32)) % period_length
    pos_keys = jax.vmap(lambda source: positions(source, row_halves, period_length))(
        sources
    ).reshape(-1)
    pos_query = positions(own_index, row_halves, period_length)
    visible = pos_keys[None, :] <= pos_query[:, None]
    query_group_count = QUERY_HEADS // KEY_VALUE_HEADS
    score_scale = 1.0 / math.sqrt(query_zig.shape[2])

    def one_head(head_id):
        query_head = lax.dynamic_index_in_dim(query_zig, head_id, 1, keepdims=False)
        key_head = lax.dynamic_index_in_dim(
            key_row_block, head_id // query_group_count, 1, keepdims=False
        )
        value_head = lax.dynamic_index_in_dim(
            value_row_block, head_id // query_group_count, 1, keepdims=False
        )
        scores = (
            lax.dot_general(
                query_head, key_head, (((1,), (1,)), ((), ())), preferred_element_type=jnp.float32
            )
            * score_scale
        )
        scores = jnp.where(visible, scores, jnp.float32(-1e30))
        head_max = jnp.max(scores, axis=1)
        weights = jnp.where(visible, jnp.exp(scores - head_max[:, None]), jnp.float32(0.0))
        head_sum = jnp.sum(weights, axis=1)
        head_out = jnp.dot(
            weights.astype(jnp.bfloat16), value_head, preferred_element_type=jnp.float32
        )
        return (head_out, head_max, head_sum)

    per_head, stat_max, stat_sum = lax.map(
        one_head, jnp.arange(query_zig.shape[1], dtype=jnp.int32)
    )
    weighted = jnp.transpose(per_head, (1, 0, 2))[None]
    return (weighted, stat_max[:, None, :], stat_sum[:, None, :])


def solution(mesh):
    in_specs = (
        P("ctx", "head", None, None),
        P("ctx", "head", None, None),
        P("ctx", "head", None, None),
    )
    out_specs = (P("ctx", None, "head", None), P("head", "ctx", None), P("head", "ctx", None))
    return jax.shard_map(local, mesh=mesh, in_specs=in_specs, out_specs=out_specs, check_vma=False)
```

profile of v0, /device:TPU:128, one launch (start us, length us, event | category | flops | bytes accessed | tf_op | source)
XLA Modules:
  0.0 216.7 jit_solution(1106706698568809709)
XLA Ops:
  2.1 14.6 %all-to-all-start.1 = ((bf16[1,64,4,128]{3,1,0,2:T(8,128)(2,1)}), bf16[1,64,4,128]{3,1,0,2:T(8,128)(2,1)S(1)}, u32[]{:S(2)}, u32[]{:S(2)}) async-start(bf16[1,64,4,128]{3,1,0,2:T(8,128)(2,1)} %copy.16), calls=%async_computation.1 | async-start | bytes 131072 | tf_op jit(solution)/shard_map/all_to_all | solution.py:31
  21.4 4.5 %all-to-all-start.2 = ((bf16[1,64,4,128]{3,1,0,2:T(8,128)(2,1)}), bf16[1,64,4,128]{3,1,0,2:T(8,128)(2,1)S(1)}, u32[]{:S(2)}, u32[]{:S(2)}) async-start(bf16[1,64,4,128]{3,1,0,2:T(8,128)(2,1)} %copy.17), calls=%async_computation.2 | async-start | bytes 131072 | tf_op jit(solution)/shard_map/all_to_all | solution.py:32
  27.7 2.7 %all-to-all-done.2 = bf16[1,64,4,128]{3,1,0,2:T(8,128)(2,1)S(1)} async-done(((bf16[1,64,4,128]{3,1,0,2:T(8,128)(2,1)}), bf16[1,64,4,128]{3,1,0,2:T(8,128)(2,1)S(1)}, u32[]{:S(2)}, u32[]{:S(2)}) %all-to-all-start.2) | async-done | bytes 65568 | tf_op jit(solution)/shard_map/all_to_all | solution.py:32
  30.5 4.7 %all-to-all-start = ((bf16[1,64,32,128]{3,1,0,2:T(8,128)(2,1)}), bf16[1,64,32,128]{3,1,0,2:T(8,128)(2,1)S(1)}, u32[]{:S(2)}, u32[]{:S(2)}) async-start(bf16[1,64,32,128]{3,1,0,2:T(8,128)(2,1)} %copy.14), calls=%async_computation | async-start | bytes 1048576 | tf_op jit(solution)/shard_map/all_to_all | solution.py:30
  41.9 7.5 %collective-permute-done.7 = bf16[256,1,128]{2,0,1:T(8,128)(2,1)S(1)} collective-permute-done((bf16[256,1,128]{2,0,1:T(8,128)(2,1)S(1)}, bf16[256,1,128]{2,0,1:T(8,128)(2,1)S(1)}, u32[]{:S(2)}, u32[]{:S(2)}) %collective-permute-start.7) | collective-permute-done | bytes 65568 | tf_op jit(solution)/shard_map/ppermute | solution.py:16
  56.4 7.2 %collective-permute-done.8 = bf16[256,1,128]{2,0,1:T(8,128)(2,1)S(1)} collective-permute-done((bf16[256,1,128]{2,0,1:T(8,128)(2,1)S(1)}, bf16[256,1,128]{2,0,1:T(8,128)(2,1)S(1)}, u32[]{:S(2)}, u32[]{:S(2)}) %collective-permute-start.8) | collective-permute-done | bytes 65568 | tf_op jit(solution)/shard_map/ppermute | solution.py:16
  66.2 2.6 %collective-permute-done.2 = bf16[256,1,128]{2,0,1:T(8,128)(2,1)S(1)} collective-permute-done((bf16[256,1,128]{2,0,1:T(8,128)(2,1)S(1)}, bf16[256,1,128]{2,0,1:T(8,128)(2,1)S(1)}, u32[]{:S(2)}, u32[]{:S(2)}) %collective-permute-start.2) | collective-permute-done | bytes 65568 | tf_op jit(solution)/shard_map/ppermute | solution.py:16
  70.6 7.2 %collective-permute-done.9 = bf16[256,1,128]{2,0,1:T(8,128)(2,1)S(1)} collective-permute-done((bf16[256,1,128]{2,0,1:T(8,128)(2,1)S(1)}, bf16[256,1,128]{2,0,1:T(8,128)(2,1)S(1)}, u32[]{:S(2)}, u32[]{:S(2)}) %collective-permute-start.9) | collective-permute-done | bytes 65568 | tf_op jit(solution)/shard_map/ppermute | solution.py:16
  80.3 2.7 %collective-permute-done.3 = bf16[256,1,128]{2,0,1:T(8,128)(2,1)S(1)} collective-permute-done((bf16[256,1,128]{2,0,1:T(8,128)(2,1)S(1)}, bf16[256,1,128]{2,0,1:T(8,128)(2,1)S(1)}, u32[]{:S(2)}, u32[]{:S(2)}) %collective-permute-start.3) | collective-permute-done | bytes 65568 | tf_op jit(solution)/shard_map/ppermute | solution.py:16
  85.0 7.2 %collective-permute-done.10 = bf16[256,1,128]{2,0,1:T(8,128)(2,1)S(1)} collective-permute-done((bf16[256,1,128]{2,0,1:T(8,128)(2,1)S(1)}, bf16[256,1,128]{2,0,1:T(8,128)(2,1)S(1)}, u32[]{:S(2)}, u32[]{:S(2)}) %collective-permute-start.10) | collective-permute-done | bytes 65568 | tf_op jit(solution)/shard_map/ppermute | solution.py:16
  94.7 2.7 %collective-permute-done.4 = bf16[256,1,128]{2,0,1:T(8,128)(2,1)S(1)} collective-permute-done((bf16[256,1,128]{2,0,1:T(8,128)(2,1)S(1)}, bf16[256,1,128]{2,0,1:T(8,128)(2,1)S(1)}, u32[]{:S(2)}, u32[]{:S(2)}) %collective-permute-start.4) | collective-permute-done | bytes 65568 | tf_op jit(solution)/shard_map/ppermute | solution.py:16
  99.4 7.2 %collective-permute-done.11 = bf16[256,1,128]{2,0,1:T(8,128)(2,1)S(1)} collective-permute-done((bf16[256,1,128]{2,0,1:T(8,128)(2,1)S(1)}, bf16[256,1,128]{2,0,1:T(8,128)(2,1)S(1)}, u32[]{:S(2)}, u32[]{:S(2)}) %collective-permute-start.11) | collective-permute-done | bytes 65568 | tf_op jit(solution)/shard_map/ppermute | solution.py:16
  109.2 2.7 %collective-permute-done.5 = bf16[256,1,128]{2,0,1:T(8,128)(2,1)S(1)} collective-permute-done((bf16[256,1,128]{2,0,1:T(8,128)(2,1)S(1)}, bf16[256,1,128]{2,0,1:T(8,128)(2,1)S(1)}, u32[]{:S(2)}, u32[]{:S(2)}) %collective-permute-start.5) | collective-permute-done | bytes 65568 | tf_op jit(solution)/shard_map/ppermute | solution.py:16
  113.7 7.1 %collective-permute-done.12 = bf16[256,1,128]{2,0,1:T(8,128)(2,1)S(1)} collective-permute-done((bf16[256,1,128]{2,0,1:T(8,128)(2,1)S(1)}, bf16[256,1,128]{2,0,1:T(8,128)(2,1)S(1)}, u32[]{:S(2)}, u32[]{:S(2)}) %collective-permute-start.12) | collective-permute-done | bytes 65568 | tf_op jit(solution)/shard_map/ppermute | solution.py:16
  126.0 9.0 %collective-permute-done.13 = bf16[256,1,128]{2,0,1:T(8,128)(2,1)S(1)} collective-permute-done((bf16[256,1,128]{2,0,1:T(8,128)(2,1)S(1)}, bf16[256,1,128]{2,0,1:T(8,128)(2,1)S(1)}, u32[]{:S(2)}, u32[]{:S(2)}) %collective-permute-start.13) | collective-permute-done | bytes 65568 | tf_op jit(solution)/shard_map/ppermute | solution.py:16
  135.6 79.9 %while.15 = (s32[]{:T(128)}, f32[8,256,128]{2,0,1:T(8,128)}, f32[8,256]{1,0:T(8,128)S(1)}, f32[8,256]{1,0:T(8,128)S(1)}, s32[8]{0:T(128)S(1)}, /*index=5*/bf16[2...) while((s32[]{:T(128)}, f32[8,256,128]{2,0,1:T(8,128)}, ...), condition=%wide.region_3.4_spmd.clone, body=%wide.region_0.3_spmd.clone.sunk | while | flops 274726400 | bytes 7834811 | solution.py:81
  140.9 4.7 %dynamic_update_slice.17 = f32[8,256,128]{2,0,1:T(8,128)} dynamic-update-slice(f32[8,256,128]{2,0,1:T(8,128)} %get-tuple-element.182, f32[1,256,128]{2,0,1:T(1,128)S(1)} %bitcast.53, s32[]{:T(128)} %get-tuple-element.181, s32[]{:T(128)} %constant.71.clone.1..sunk, s32[]{:T(128)} %constant.71.clone.1..sunk) | dynamic-update-slice | bytes 262148 | tf_op jit(solution)/shard_map/while/body/jit(dynamic_update_index_in_dim)/dynamic_update_slice | solution.py:81
  150.9 4.7 %dynamic_update_slice.17 = f32[8,256,128]{2,0,1:T(8,128)} dynamic-update-slice(f32[8,256,128]{2,0,1:T(8,128)} %get-tuple-element.182, f32[1,256,128]{2,0,1:T(1,128)S(1)} %bitcast.53, s32[]{:T(128)} %get-tuple-element.181, s32[]{:T(128)} %constant.71.clone.1..sunk, s32[]{:T(128)} %constant.71.clone.1..sunk) | dynamic-update-slice | bytes 262148 | tf_op jit(solution)/shard_map/while/body/jit(dynamic_update_index_in_dim)/dynamic_update_slice | solution.py:81
  160.9 4.7 %dynamic_update_slice.17 = f32[8,256,128]{2,0,1:T(8,128)} dynamic-update-slice(f32[8,256,128]{2,0,1:T(8,128)} %get-tuple-element.182, f32[1,256,128]{2,0,1:T(1,128)S(1)} %bitcast.53, s32[]{:T(128)} %get-tuple-element.181, s32[]{:T(128)} %constant.71.clone.1..sunk, s32[]{:T(128)} %constant.71.clone.1..sunk) | dynamic-update-slice | bytes 262148 | tf_op jit(solution)/shard_map/while/body/jit(dynamic_update_index_in_dim)/dynamic_update_slice | solution.py:81
  170.9 4.7 %dynamic_update_slice.17 = f32[8,256,128]{2,0,1:T(8,128)} dynamic-update-slice(f32[8,256,128]{2,0,1:T(8,128)} %get-tuple-element.182, f32[1,256,128]{2,0,1:T(1,128)S(1)} %bitcast.53, s32[]{:T(128)} %get-tuple-element.181, s32[]{:T(128)} %constant.71.clone.1..sunk, s32[]{:T(128)} %constant.71.clone.1..sunk) | dynamic-update-slice | bytes 262148 | tf_op jit(solution)/shard_map/while/body/jit(dynamic_update_index_in_dim)/dynamic_update_slice | solution.py:81
  180.9 4.7 %dynamic_update_slice.17 = f32[8,256,128]{2,0,1:T(8,128)} dynamic-update-slice(f32[8,256,128]{2,0,1:T(8,128)} %get-tuple-element.182, f32[1,256,128]{2,0,1:T(1,128)S(1)} %bitcast.53, s32[]{:T(128)} %get-tuple-element.181, s32[]{:T(128)} %constant.71.clone.1..sunk, s32[]{:T(128)} %constant.71.clone.1..sunk) | dynamic-update-slice | bytes 262148 | tf_op jit(solution)/shard_map/while/body/jit(dynamic_update_index_in_dim)/dynamic_update_slice | solution.py:81
  190.9 4.7 %dynamic_update_slice.17 = f32[8,256,128]{2,0,1:T(8,128)} dynamic-update-slice(f32[8,256,128]{2,0,1:T(8,128)} %get-tuple-element.182, f32[1,256,128]{2,0,1:T(1,128)S(1)} %bitcast.53, s32[]{:T(128)} %get-tuple-element.181, s32[]{:T(128)} %constant.71.clone.1..sunk, s32[]{:T(128)} %constant.71.clone.1..sunk) | dynamic-update-slice | bytes 262148 | tf_op jit(solution)/shard_map/while/body/jit(dynamic_update_index_in_dim)/dynamic_update_slice | solution.py:81
  200.8 4.7 %dynamic_update_slice.17 = f32[8,256,128]{2,0,1:T(8,128)} dynamic-update-slice(f32[8,256,128]{2,0,1:T(8,128)} %get-tuple-element.182, f32[1,256,128]{2,0,1:T(1,128)S(1)} %bitcast.53, s32[]{:T(128)} %get-tuple-element.181, s32[]{:T(128)} %constant.71.clone.1..sunk, s32[]{:T(128)} %constant.71.clone.1..sunk) | dynamic-update-slice | bytes 262148 | tf_op jit(solution)/shard_map/while/body/jit(dynamic_update_index_in_dim)/dynamic_update_slice | solution.py:81
  210.8 4.7 %dynamic_update_slice.17 = f32[8,256,128]{2,0,1:T(8,128)} dynamic-update-slice(f32[8,256,128]{2,0,1:T(8,128)} %get-tuple-element.182, f32[1,256,128]{2,0,1:T(1,128)S(1)} %bitcast.53, s32[]{:T(128)} %get-tuple-element.181, s32[]{:T(128)} %constant.71.clone.1..sunk, s32[]{:T(128)} %constant.71.clone.1..sunk) | dynamic-update-slice | bytes 262148 | tf_op jit(solution)/shard_map/while/body/jit(dynamic_update_index_in_dim)/dynamic_update_slice | solution.py:81
  (98 shorter events, 73.4 us)
Async XLA Ops:
  2.1 19.3 %all-to-all-start.1 = ((bf16[1,64,4,128]{3,1,0,2:T(8,128)(2,1)}), bf16[1,64,4,128]{3,1,0,2:T(8,128)(2,1)S(1)}, u32[]{:S(2)}, u32[]{:S(2)}) async-start(bf16[1,64,4,128]{3,1,0,2:T(8,128)(2,1)} %copy.16), calls=%async_computation.1 | async-start | bytes 131072 | tf_op jit(solution)/shard_map/all_to_all | solution.py:31
  21.4 9.1 %all-to-all-start.2 = ((bf16[1,64,4,128]{3,1,0,2:T(8,128)(2,1)}), bf16[1,64,4,128]{3,1,0,2:T(8,128)(2,1)S(1)}, u32[]{:S(2)}, u32[]{:S(2)}) async-start(bf16[1,64,4,128]{3,1,0,2:T(8,128)(2,1)} %copy.17), calls=%async_computation.2 | async-start | bytes 131072 | tf_op jit(solution)/shard_map/all_to_all | solution.py:32
  25.8 14.1 %collective-permute-start = (bf16[256,1,128]{2,0,1:T(8,128)(2,1)S(1)}, bf16[256,1,128]{2,0,1:T(8,128)(2,1)S(1)}, u32[]{:S(2)}, u32[]{:S(2)}) collective-permute-start(bf16[256,1,128]{2,0,1:T(8,128)(2,1)S(1)} %bitcast.57), channel_id=1, source_target_pairs={{1020,0},{0,4},{4,8},{8,12},{12,16},{16,20},{20,24},{24,28},{28,32... | collective-permute-start | bytes 196616 | tf_op jit(solution)/shard_map/ppermute | solution.py:16
  30.5 105.1 %all-to-all-start = ((bf16[1,64,32,128]{3,1,0,2:T(8,128)(2,1)}), bf16[1,64,32,128]{3,1,0,2:T(8,128)(2,1)S(1)}, u32[]{:S(2)}, u32[]{:S(2)}) async-start(bf16[1,64,32,128]{3,1,0,2:T(8,128)(2,1)} %copy.14), calls=%async_computation | async-start | bytes 1048576 | tf_op jit(solution)/shard_map/all_to_all | solution.py:30
  35.1 14.3 %collective-permute-start.7 = (bf16[256,1,128]{2,0,1:T(8,128)(2,1)S(1)}, bf16[256,1,128]{2,0,1:T(8,128)(2,1)S(1)}, u32[]{:S(2)}, u32[]{:S(2)}) collective-permute-start(bf16[256,1,128]{2,0,1:T(8,128)(2,1)S(1)} %bitcast.59), channel_id=1, source_target_pairs={{1020,0},{0,4},{4,8},{8,12},{12,16},{16,20},{20,24},{24,28},{28,32... | collective-permute-start | bytes 196616 | tf_op jit(solution)/shard_map/ppermute | solution.py:16
  39.9 14.5 %collective-permute-start.1 = (bf16[256,1,128]{2,0,1:T(8,128)(2,1)S(1)}, bf16[256,1,128]{2,0,1:T(8,128)(2,1)S(1)}, u32[]{:S(2)}, u32[]{:S(2)}) collective-permute-start(bf16[256,1,128]{2,0,1:T(8,128)(2,1)S(1)} %collective-permute-done), channel_id=1, source_target_pairs={{1020,0},{0,4},{4,8},{8,12},{12,16},{16,20},{20,24},{24,28},{28,32... | collective-permute-start | bytes 196616 | tf_op jit(solution)/shard_map/ppermute | solution.py:16
  49.4 14.2 %collective-permute-start.8 = (bf16[256,1,128]{2,0,1:T(8,128)(2,1)S(1)}, bf16[256,1,128]{2,0,1:T(8,128)(2,1)S(1)}, u32[]{:S(2)}, u32[]{:S(2)}) collective-permute-start(bf16[256,1,128]{2,0,1:T(8,128)(2,1)S(1)} %collective-permute-done.7), channel_id=1, source_target_pairs={{1020,0},{0,4},{4,8},{8,12},{12,16},{16,20},{20,24},{24,28},{28,32... | collective-permute-start | bytes 196616 | tf_op jit(solution)/shard_map/ppermute | solution.py:16
  54.4 14.3 %collective-permute-start.2 = (bf16[256,1,128]{2,0,1:T(8,128)(2,1)S(1)}, bf16[256,1,128]{2,0,1:T(8,128)(2,1)S(1)}, u32[]{:S(2)}, u32[]{:S(2)}) collective-permute-start(bf16[256,1,128]{2,0,1:T(8,128)(2,1)S(1)} %collective-permute-done.1), channel_id=1, source_target_pairs={{1020,0},{0,4},{4,8},{8,12},{12,16},{16,20},{20,24},{24,28},{28,32... | collective-permute-start | bytes 196616 | tf_op jit(solution)/shard_map/ppermute | solution.py:16
  63.6 14.2 %collective-permute-start.9 = (bf16[256,1,128]{2,0,1:T(8,128)(2,1)S(1)}, bf16[256,1,128]{2,0,1:T(8,128)(2,1)S(1)}, u32[]{:S(2)}, u32[]{:S(2)}) collective-permute-start(bf16[256,1,128]{2,0,1:T(8,128)(2,1)S(1)} %collective-permute-done.8), channel_id=1, source_target_pairs={{1020,0},{0,4},{4,8},{8,12},{12,16},{16,20},{20,24},{24,28},{28,32... | collective-permute-start | bytes 196616 | tf_op jit(solution)/shard_map/ppermute | solution.py:16
  68.7 14.4 %collective-permute-start.3 = (bf16[256,1,128]{2,0,1:T(8,128)(2,1)S(1)}, bf16[256,1,128]{2,0,1:T(8,128)(2,1)S(1)}, u32[]{:S(2)}, u32[]{:S(2)}) collective-permute-start(bf16[256,1,128]{2,0,1:T(8,128)(2,1)S(1)} %collective-permute-done.2), channel_id=1, source_target_pairs={{1020,0},{0,4},{4,8},{8,12},{12,16},{16,20},{20,24},{24,28},{28,32... | collective-permute-start | bytes 196616 | tf_op jit(solution)/shard_map/ppermute | solution.py:16
  77.8 14.4 %collective-permute-start.10 = (bf16[256,1,128]{2,0,1:T(8,128)(2,1)S(1)}, bf16[256,1,128]{2,0,1:T(8,128)(2,1)S(1)}, u32[]{:S(2)}, u32[]{:S(2)}) collective-permute-start(bf16[256,1,128]{2,0,1:T(8,128)(2,1)S(1)} %collective-permute-done.9), channel_id=1, source_target_pairs={{1020,0},{0,4},{4,8},{8,12},{12,16},{16,20},{20,24},{24,28},{28,32... | collective-permute-start | bytes 196616 | tf_op jit(solution)/shard_map/ppermute | solution.py:16
  83.1 14.4 %collective-permute-start.4 = (bf16[256,1,128]{2,0,1:T(8,128)(2,1)S(1)}, bf16[256,1,128]{2,0,1:T(8,128)(2,1)S(1)}, u32[]{:S(2)}, u32[]{:S(2)}) collective-permute-start(bf16[256,1,128]{2,0,1:T(8,128)(2,1)S(1)} %collective-permute-done.3), channel_id=1, source_target_pairs={{1020,0},{0,4},{4,8},{8,12},{12,16},{16,20},{20,24},{24,28},{28,32... | collective-permute-start | bytes 196616 | tf_op jit(solution)/shard_map/ppermute | solution.py:16
  92.2 14.4 %collective-permute-start.11 = (bf16[256,1,128]{2,0,1:T(8,128)(2,1)S(1)}, bf16[256,1,128]{2,0,1:T(8,128)(2,1)S(1)}, u32[]{:S(2)}, u32[]{:S(2)}) collective-permute-start(bf16[256,1,128]{2,0,1:T(8,128)(2,1)S(1)} %collective-permute-done.10), channel_id=1, source_target_pairs={{1020,0},{0,4},{4,8},{8,12},{12,16},{16,20},{20,24},{24,28},{28,32... | collective-permute-start | bytes 196616 | tf_op jit(solution)/shard_map/ppermute | solution.py:16
  97.5 14.3 %collective-permute-start.5 = (bf16[256,1,128]{2,0,1:T(8,128)(2,1)S(1)}, bf16[256,1,128]{2,0,1:T(8,128)(2,1)S(1)}, u32[]{:S(2)}, u32[]{:S(2)}) collective-permute-start(bf16[256,1,128]{2,0,1:T(8,128)(2,1)S(1)} %collective-permute-done.4), channel_id=1, source_target_pairs={{1020,0},{0,4},{4,8},{8,12},{12,16},{16,20},{20,24},{24,28},{28,32... | collective-permute-start | bytes 196616 | tf_op jit(solution)/shard_map/ppermute | solution.py:16
  106.6 14.3 %collective-permute-start.12 = (bf16[256,1,128]{2,0,1:T(8,128)(2,1)S(1)}, bf16[256,1,128]{2,0,1:T(8,128)(2,1)S(1)}, u32[]{:S(2)}, u32[]{:S(2)}) collective-permute-start(bf16[256,1,128]{2,0,1:T(8,128)(2,1)S(1)} %collective-permute-done.11), channel_id=1, source_target_pairs={{1020,0},{0,4},{4,8},{8,12},{12,16},{16,20},{20,24},{24,28},{28,32... | collective-permute-start | bytes 196616 | tf_op jit(solution)/shard_map/ppermute | solution.py:16
  111.8 14.1 %collective-permute-start.6 = (bf16[256,1,128]{2,0,1:T(8,128)(2,1)S(1)}, bf16[256,1,128]{2,0,1:T(8,128)(2,1)S(1)}, u32[]{:S(2)}, u32[]{:S(2)}) collective-permute-start(bf16[256,1,128]{2,0,1:T(8,128)(2,1)S(1)} %collective-permute-done.5), channel_id=1, source_target_pairs={{1020,0},{0,4},{4,8},{8,12},{12,16},{16,20},{20,24},{24,28},{28,32... | collective-permute-start | bytes 196616 | tf_op jit(solution)/shard_map/ppermute | solution.py:16
  120.9 14.1 %collective-permute-start.13 = (bf16[256,1,128]{2,0,1:T(8,128)(2,1)S(1)}, bf16[256,1,128]{2,0,1:T(8,128)(2,1)S(1)}, u32[]{:S(2)}, u32[]{:S(2)}) collective-permute-start(bf16[256,1,128]{2,0,1:T(8,128)(2,1)S(1)} %collective-permute-done.12), channel_id=1, source_target_pairs={{1020,0},{0,4},{4,8},{8,12},{12,16},{16,20},{20,24},{24,28},{28,32... | collective-permute-start | bytes 196616 | tf_op jit(solution)/shard_map/ppermute | solution.py:16
where the time goes:
time: 219 us; the launch traced here: 217 us
  waiting for transfers between devices  74.1 us (34%)
  local copies, waits for them, and re-layouts  53.8 us (25%)
  starting transfers between devices  50.4 us (23%)
  matrix products  17.2 us (8%)
  loops' own time  15.8 us (7%)
  other arithmetic  4.59 us (2%)
    ppermute x14, waiting for transfers between devices, shifted(): return lax.ppermute(block, axis, route)  70.4 us
    dynamic_update_slice x24, local copies, waits for them, and re-layouts, local(): lax.map(one_head, jnp.arange(query_zig.shape[1], dtype=jnp.int32))  37.7 us
    ppermute x14, starting transfers between devices, shifted(): return lax.ppermute(block, axis, route)  26.7 us
    another operation x1, loops' own time, local(): lax.map(one_head, jnp.arange(query_zig.shape[1], dtype=jnp.int32))  15.8 us
    all_to_all x1, starting transfers between devices, local(): lax.all_to_all(keys, 'head', split_axis=2, concat_axis=1, tiled=True)  14.6 us
    dot_general x8, matrix products, one_head(): jnp.dot(weights.astype(jnp.bfloat16), value_head, preferred_element_type=...  12.8 us
    unnamed x18, local copies, waits for them, and re-layouts  9.47 us
    dynamic_slice x8, local copies, waits for them, and re-layouts, local(): lax.map(one_head, jnp.arange(query_zig.shape[1], dtype=jnp.int32))  4.69 us
  transfers between devices with their start and end apart: 17, of which 16 were waited for; matrix products, arithmetic and copies ran while one was open for 4% of the time, Pallas kernels for 0%

commit v1 on v0

v1 whole, which is shorter than its diff:
```python
import functools
import math

import jax
import jax.numpy as jnp
from jax import lax
from jax.experimental import pallas as pl
from jax.experimental.pallas import tpu as pltpu
from jax.sharding import PartitionSpec as P

MESH = pl.DeviceIdType.MESH
HALF = 128
ROWS = 64
HEADS = 4
GROUP = 8
WIDTH = 128
BLOCK = 128
PAIRS = 256
WIN = 8


def gather_kernel(q_ref, k_ref, v_ref, q_out, x_out, wide, stage,
                  q_send, q_recv, q_own, s_send, s_recv, s_own, e_send, c_send, b_send, d_send, x_recv, w_send):
    c = lax.axis_index("ctx")
    h = lax.axis_index("head")
    core = lax.rem(c, 2)
    place = lax.rem(c, BLOCK)
    back = BLOCK - place
    crosser = back <= 7
    over = c >= BLOCK
    base = lax.select(over, 0, BLOCK)
    x_core = lax.select(back == 7, 0, lax.rem(back, 2))
    x_j = lax.select(back == 7, 7, back + lax.rem(back, 2))
    near = place < 2
    last = place >= BLOCK - 2
    sibling = c + 1 - 2 * core

    def wrapped(pair):
        return lax.rem(pair + PAIRS, PAIRS)

    bar = pltpu.get_barrier_semaphore()

    def greet(pair, head):
        pl.semaphore_signal(bar, inc=1, device_id=(pair, head), device_id_type=MESH)

    for s in range(1, HEADS):
        greet(c, lax.rem(h + s, HEADS))
    greet(sibling, h)

    @pl.when(jnp.logical_not(near))
    def _():
        greet(c - 2, h)

        @pl.when(core == 0)
        def _():
            greet(c - 1, h)

    @pl.when(near)
    def _():
        for j in (2, 4, 6, 7):
            @pl.when((j != 7) | (core == 0))
            def _():
                for r in range(HEADS):
                    greet(wrapped(c - j), r)

    for n, ref in enumerate((k_ref, v_ref)):
        wide[n] = ref[...].astype(jnp.float32)
    for n in range(2):
        for head in range(HEADS):
            stage[n, head] = wide[n, pl.ds(head, ROWS, stride=HEADS), :].astype(jnp.bfloat16)

    one, none = jnp.int32(1), jnp.int32(0)
    targets = (4 + lax.select(last, none, one) + lax.select(last | (core == 0), none, one)
               + lax.select(crosser, one, none) * 4)
    pl.semaphore_wait(bar, targets)

    def remote(src, dst, send, recv, pair, head):
        return pltpu.make_async_remote_copy(src_ref=src, dst_ref=dst, send_sem=send, recv_sem=recv,
                                            device_id=(pair, head), device_id_type=MESH)

    def own_rows(head):
        return x_out.at[:, head // 2, 0, pl.ds(lax.rem(head, 2) * ROWS, ROWS), :]

    kv_copies = []
    for s in (3, 2, 1):
        to = lax.rem(h + s, HEADS)
        copy = remote(stage.at[:, to], own_rows(h), s_send.at[s], s_recv.at[h], c, to)
        copy.start()
        kv_copies.append(copy)
    kv_own = pltpu.make_async_copy(stage.at[:, h], own_rows(h), s_own)
    kv_own.start()

    half_to = lax.select(over, 1 - h // 2, h // 2)

    def cross_copy(to):
        return remote(stage.at[:, to], x_out.at[:, half_to, x_j, pl.ds(lax.rem(h, 2) * ROWS, ROWS), :],
                      w_send.at[to], x_recv.at[x_j, half_to], base + x_core, to)

    @pl.when(crosser)
    def _():
        for to in range(HEADS):
            cross_copy(to).start()

    q_copies = []
    for s in (3, 2, 1):
        to = lax.rem(h + s, HEADS)
        copy = remote(q_ref.at[:, to], q_out.at[h], q_send.at[s], q_recv.at[h], c, to)
        copy.start()
        q_copies.append(copy)
    q_mine = pltpu.make_async_copy(q_ref.at[:, h], q_out.at[h], q_own)
    q_mine.start()

    kv_own.wait()

    def arrive(head):
        @pl.when(h != head)
        def _():
            remote(stage.at[:, head], own_rows(head), e_send, s_recv.at[head], c, h).wait_recv()

    def block(half, j):
        return x_out.at[:, half, j]

    def along(j, half):
        return remote(block(half, j), block(half, j + 2), c_send.at[j // 2, half], x_recv.at[j + 2, half],
                      wrapped(c + 2), h)

    def beside(j, half):
        j_to = j + 1 - 2 * core
        return remote(block(half, j), block(half, j_to), b_send.at[j // 2, half], x_recv.at[j_to, half], sibling, h)

    def ahead(half):
        return remote(block(half, 6), block(half, 7), d_send.at[half], x_recv.at[7, half], wrapped(c + 1), h)

    def landed(j, half):
        remote(block(half, j), block(half, j), e_send, x_recv.at[j, half], c, h).wait_recv()

    for j in (0, 2, 4, 6):
        for half in range(2):
            if j:
                landed(j, half)
            else:
                arrive(2 * half)
                arrive(2 * half + 1)
            if j < 6:
                @pl.when(jnp.logical_not(last))
                def _():
                    along(j, half).start()
            else:
                @pl.when(jnp.logical_not(last) & (core == 1))
                def _():
                    ahead(half).start()
            if j:
                beside(j, half).start()
            else:
                @pl.when(core == 0)
                def _():
                    beside(0, half).start()
    for j in (1, 3, 5, 7):
        for half in range(2):
            landed(j, half)
    for s in (1, 2, 3):
        head = lax.rem(h + s, HEADS)
        remote(q_ref.at[:, head], q_out.at[head], e_send, q_recv.at[head], c, h).wait_recv()
    q_mine.wait()
    for copy in kv_copies + q_copies:
        copy.wait_send()

    @pl.when(crosser)
    def _():
        for to in range(HEADS):
            cross_copy(to).wait_send()

    for half in range(2):
        @pl.when(jnp.logical_not(last))
        def _():
            for j in (0, 2, 4):
                along(j, half).wait_send()

        @pl.when(jnp.logical_not(last) & (core == 1))
        def _():
            ahead(half).wait_send()

        @pl.when(core == 0)
        def _():
            beside(0, half).wait_send()
        for j in (2, 4, 6):
            beside(j, half).wait_send()


def gather(q, k, v):
    dma = pltpu.SemaphoreType.DMA
    any_space = pl.BlockSpec(memory_space=pl.ANY)
    vmem = pl.BlockSpec(memory_space=pltpu.VMEM)
    return pl.pallas_call(
        gather_kernel,
        out_shape=(
            jax.ShapeDtypeStruct((HEADS, ROWS, GROUP, WIDTH), jnp.bfloat16),
            jax.ShapeDtypeStruct((2, 2, WIN, HALF, WIDTH), jnp.bfloat16),
        ),
        in_specs=[any_space, vmem, vmem],
        out_specs=(any_space, any_space),
        scratch_shapes=[
            pltpu.VMEM((2, ROWS * HEADS, WIDTH), jnp.float32),
            pltpu.VMEM((2, HEADS, ROWS, WIDTH), jnp.bfloat16),
            dma((4,)), dma((4,)), dma(()), dma((4,)), dma((4,)), dma(()), dma(()), dma((3, 2)), dma((4, 2)), dma((2,)),
            dma((8, 2)), dma((4,)),
        ],
        compiler_params=pltpu.CompilerParams(collective_id=0, has_side_effects=True),
        name="gather",
    )(q, k, v)


CHUNK = 256
TOKENS = CHUNK // GROUP
SCALE = 1.0 / math.sqrt(WIDTH)
LOG2E = math.log2(math.e)
LOW = -1e30


def nt_dot(a, b):
    return lax.dot_general(a, b, (((1,), (1,)), ((), ())), preferred_element_type=jnp.float32)


def attend_kernel(q_ref, x_ref, o_ref, m_ref, l_ref, stats):
    step = pl.program_id(0)
    half_steps = HALF // TOKENS
    c = lax.axis_index("ctx")
    token0 = lax.rem(step, half_steps) * TOKENS
    half = step // half_steps
    upper = c >= BLOCK
    place = lax.rem(c, BLOCK)
    special = place < 4
    q = q_ref[...]

    @pl.when(step == 0)
    def _():
        stats[...] = jnp.zeros_like(stats)

    def causal():
        row = token0 + lax.broadcasted_iota(jnp.int32, (CHUNK, HALF), 0) // GROUP
        return lax.broadcasted_iota(jnp.int32, (CHUNK, HALF), 1) <= row

    def put_stats(peak, norm):
        lane = lax.broadcasted_iota(jnp.int32, (TOKENS, GROUP, HALF), 2)
        want = token0 + lax.broadcasted_iota(jnp.int32, (TOKENS, GROUP, HALF), 0)
        hit = lane == want
        for n, value in enumerate((peak, norm)):
            wide = jnp.broadcast_to(value, (CHUNK, HALF)).reshape(TOKENS, GROUP, HALF)
            stats[n, half] += jnp.sum(jnp.where(hit, wide, 0.0), axis=0)

    def whole(diagonal, *ranges):
        pieces = [(diagonal, diagonal + 1), *(r for r in ranges if r[1] > r[0])]
        s = []
        for n, (a, b) in enumerate(pieces):
            one = nt_dot(q, x_ref[0, a:b].reshape(-1, WIDTH))
            s.append(one if n else jnp.where(causal(), one, LOW))
        peak = functools.reduce(jnp.maximum, [jnp.max(one, axis=1, keepdims=True) for one in s])
        norm, out = 0.0, 0.0
        for one, (a, b) in zip(s, pieces):
            p = jnp.exp2((one - peak) * (SCALE * LOG2E))
            norm += jnp.sum(p, axis=1, keepdims=True)
            out += jnp.dot(p.astype(jnp.bfloat16), x_ref[1, a:b].reshape(-1, WIDTH),
                           preferred_element_type=jnp.float32)
        o_ref[...] = out
        put_stats(peak * SCALE, norm)

    cases = {(0, None): ([(1, WIN)], [(0, WIN)]), (1, None): ([(1, 2 * WIN)], [])}
    for two in range(0, WIN, 2):
        cases[0, two // 2] = ([(1, two + 1)], [(0, WIN), (WIN + two + 1, 2 * WIN)])
        cases[1, two // 2] = ([(1, WIN + two + 1)], [(two + 1, WIN)])
    for (side, at), by_half in cases.items():
        here = (upper == (side == 1)) & (jnp.logical_not(special) if at is None else place == at)
        for which, ranges in enumerate(by_half):
            @pl.when(here & (half == which))
            def _():
                whole(which * WIN, *ranges)

    @pl.when(step == 2 * half_steps - 1)
    def _():
        for n, ref in enumerate((m_ref, l_ref)):
            for side in range(2):
                for g in range(GROUP):
                    ref[g, :, pl.ds(side * HALF, HALF)] = stats[n, side, pl.ds(g, 1), :]


def attend(q, x):
    rows = q.shape[0]
    return pl.pallas_call(
        attend_kernel,
        grid=(rows // CHUNK,),
        out_shape=(
            jax.ShapeDtypeStruct((rows, WIDTH), jnp.float32),
            jax.ShapeDtypeStruct((GROUP, 1, 2 * HALF), jnp.float32),
            jax.ShapeDtypeStruct((GROUP, 1, 2 * HALF), jnp.float32),
        ),
        in_specs=[
            pl.BlockSpec((CHUNK, WIDTH), lambda i: (i, 0)),
            pl.BlockSpec((2, 2 * WIN, HALF, WIDTH), lambda i: (0, 0, 0, 0)),
        ],
        out_specs=(
            pl.BlockSpec((CHUNK, WIDTH), lambda i: (i, 0)),
            pl.BlockSpec((GROUP, 1, 2 * HALF), lambda i: (0, 0, 0)),
            pl.BlockSpec((GROUP, 1, 2 * HALF), lambda i: (0, 0, 0)),
        ),
        scratch_shapes=[
            pltpu.VMEM((2, 2, GROUP, HALF), jnp.float32),
        ],
        name="attend",
    )(q, x)


def local(queries, keys, values):
    q = queries.reshape(ROWS, HEADS, GROUP, WIDTH)
    k = keys.reshape(ROWS * HEADS, WIDTH)
    v = values.reshape(ROWS * HEADS, WIDTH)
    q_all, x = gather(q, k, v)
    out, peak, norm = attend(q_all.reshape(-1, WIDTH), x.reshape(2, 2 * WIN, HALF, WIDTH))
    return out.reshape(1, 2 * HALF, GROUP, WIDTH), peak, norm


def solution(mesh):
    spec = P("ctx", "head", None, None)
    out_specs = (P("ctx", None, "head", None), P("head", "ctx", None), P("head", "ctx", None))
    return jax.shard_map(local, mesh=mesh, in_specs=(spec, spec, spec), out_specs=out_specs, check_vma=False)
```

time: 219 us -> 69.1 us (0.32)
  the two profiles are of different devices: /device:TPU:128 before, /device:TPU:33 now
where the time goes in v1:
time: 69.1 us; the launch traced here: 68.6 us
  Pallas kernels  67.9 us (98%)
    pallas_call x1, Pallas kernels, gather(): pl.pallas_call(gather_kernel, out_shape=(jax.ShapeDtypeStruct((HEADS, ROW...  59 us
    pallas_call x1, Pallas kernels, attend(): pl.pallas_call(attend_kernel, grid=(rows // CHUNK,), out_shape=(jax.Shape...  8.9 us

profile of v1, /device:TPU:33, one launch (start us, length us, event | category | flops | bytes accessed | tf_op | source)
XLA Modules:
  0.0 68.6 jit_solution(7146144844515325793)
XLA Ops:
  0.6 59.0 %gather.1 = (bf16[4,64,8,128]{3,2,1,0:T(8,128)(2,1)}, bf16[2,2,8,128,128]{4,3,2,1,0:T(8,128)(2,1)}) custom-call(bf16[64,4,8,128]{3,2,1,0:T(8,128)(2,1)} %bitcast.8, bf16[256,128]{1,0:T(8,128)(2,1)} %bitcast.9, bf16[256,128]{1,0:T(8,128)(2,1)} %bitcast.10), custom_call_target="tpu_custom_call" | custom-call | tf_op jit(solution)/shard_map/gather/pallas_call | solution.py:194
  59.7 8.9 %attend.1 = (f32[2048,128]{1,0:T(8,128)}, f32[8,1,256]{2,1,0:T(1,128)}, f32[8,1,256]{2,1,0:T(1,128)}) custom-call(bf16[2048,128]{1,0:T(8,128)(2,1)} %bitcast.7, bf16[2,16,128,128]{3,2,1,0:T(8,128)(2,1)} %bitcast.6), custom_call_target="tpu_custom_call" | custom-call | tf_op jit(solution)/shard_map/attend/pallas_call | solution.py:288

commit v2 on v1

--- a/solution.py
+++ b/solution.py
@@ -20,7 +20,8 @@
 
 
 def gather_kernel(q_ref, k_ref, v_ref, q_out, x_out, wide, stage,
-                  q_send, q_recv, q_own, s_send, s_recv, s_own, e_send, c_send, b_send, d_send, x_recv, w_send):
+                  q_send, q_recv, q_own, s_send, s_recv, s_own, e_send, c_send, b_send, d_send, x_recv, w_send,
+                  r_recv, r_send, relay, ready):
     c = lax.axis_index("ctx")
     h = lax.axis_index("head")
     core = lax.rem(c, 2)
@@ -28,13 +29,20 @@
     back = BLOCK - place
     crosser = back <= 7
     over = c >= BLOCK
-    base = lax.select(over, 0, BLOCK)
+    across = lax.select(over, c - BLOCK, c + BLOCK)
+    base = lax.select(over, BLOCK, 0)
     x_core = lax.select(back == 7, 0, lax.rem(back, 2))
     x_j = lax.select(back == 7, 7, back + lax.rem(back, 2))
     near = place < 2
     last = place >= BLOCK - 2
     sibling = c + 1 - 2 * core
 
+    def both(j):
+        return (over & (c - j >= BLOCK - 3)) | (c < 4)
+
+    def both_next(j):
+        return (over & (c - j >= BLOCK - 3)) | (c < 2)
+
     def wrapped(pair):
         return lax.rem(pair + PAIRS, PAIRS)
 
@@ -55,13 +63,11 @@
         def _():
             greet(c - 1, h)
 
-    @pl.when(near)
-    def _():
-        for j in (2, 4, 6, 7):
-            @pl.when((j != 7) | (core == 0))
-            def _():
-                for r in range(HEADS):
-                    greet(wrapped(c - j), r)
+    @pl.when(crosser)
+    def _():
+        for r in range(HEADS):
+            greet(across, r)
+        greet(base + x_core, h)
 
     for n, ref in enumerate((k_ref, v_ref)):
         wide[n] = ref[...].astype(jnp.float32)
@@ -71,8 +77,15 @@
 
     one, none = jnp.int32(1), jnp.int32(0)
     targets = (4 + lax.select(last, none, one) + lax.select(last | (core == 0), none, one)
-               + lax.select(crosser, one, none) * 4)
+               + lax.select(crosser, one, none) * 4 + lax.select(near, one, none) * (4 - core))
     pl.semaphore_wait(bar, targets)
+
+    @pl.when(near)
+    def _():
+        for j in (2, 4, 6, 7):
+            @pl.when((j != 7) | (core == 0))
+            def _():
+                pl.semaphore_signal(ready, inc=1, device_id=(wrapped(c - j + BLOCK), h), device_id_type=MESH)
 
     def remote(src, dst, send, recv, pair, head):
         return pltpu.make_async_remote_copy(src_ref=src, dst_ref=dst, send_sem=send, recv_sem=recv,
@@ -93,10 +106,16 @@
     half_to = lax.select(over, 1 - h // 2, h // 2)
 
     def cross_copy(to):
-        return remote(stage.at[:, to], x_out.at[:, half_to, x_j, pl.ds(lax.rem(h, 2) * ROWS, ROWS), :],
-                      w_send.at[to], x_recv.at[x_j, half_to], base + x_core, to)
-
-    @pl.when(crosser)
+        return remote(stage.at[:, to], relay.at[:, half_to, pl.ds(lax.rem(h, 2) * ROWS, ROWS), :],
+                      w_send.at[to], r_recv.at[half_to], across, to)
+
+    def relay_copy(half):
+        return remote(relay.at[:, half], x_out.at[:, half, x_j], r_send.at[half], x_recv.at[x_j, half],
+                      base + x_core, h)
+
+    crosses = crosser & (over | (back <= 3) | (h < 2))
+
+    @pl.when(crosses)
     def _():
         for to in range(HEADS):
             cross_copy(to).start()
@@ -134,30 +153,51 @@
     def landed(j, half):
         remote(block(half, j), block(half, j), e_send, x_recv.at[j, half], c, h).wait_recv()
 
+    def seen(half, where):
+        return where if half else True
+
+    def relays(half):
+        return crosser & seen(half, jnp.logical_not(over) | (back <= 3))
+
+    def chain(j, half, act):
+        if j < 6:
+            @pl.when(jnp.logical_not(last) & seen(half, both_next(j)))
+            def _():
+                act(along(j, half))
+        else:
+            @pl.when(jnp.logical_not(last) & (core == 1) & seen(half, both_next(j)))
+            def _():
+                act(ahead(half))
+
+        @pl.when(seen(half, both(j)) & ((core == 0) | (j > 0)))
+        def _():
+            act(beside(j, half))
+
     for j in (0, 2, 4, 6):
         for half in range(2):
             if j:
-                landed(j, half)
+                @pl.when(seen(half, both(j)))
+                def _():
+                    landed(j, half)
             else:
                 arrive(2 * half)
                 arrive(2 * half + 1)
-            if j < 6:
-                @pl.when(jnp.logical_not(last))
+            chain(j, half, lambda copy: copy.start())
+        if j == 0:
+            @pl.when(crosser)
+            def _():
+                pl.semaphore_wait(ready, 1)
+
+            for half in range(2):
+                @pl.when(relays(half))
                 def _():
-                    along(j, half).start()
-            else:
-                @pl.when(jnp.logical_not(last) & (core == 1))
-                def _():
-                    ahead(half).start()
-            if j:
-                beside(j, half).start()
-            else:
-                @pl.when(core == 0)
-                def _():
-                    beside(0, half).start()
+                    remote(relay.at[:, half], relay.at[:, half], e_send, r_recv.at[half], c, h).wait_recv()
+                    relay_copy(half).start()
     for j in (1, 3, 5, 7):
         for half in range(2):
-            landed(j, half)
+            @pl.when(seen(half, both(j)))
+            def _():
+                landed(j, half)
     for s in (1, 2, 3):
         head = lax.rem(h + s, HEADS)
         remote(q_ref.at[:, head], q_out.at[head], e_send, q_recv.at[head], c, h).wait_recv()
@@ -165,26 +205,19 @@
     for copy in kv_copies + q_copies:
         copy.wait_send()
 
-    @pl.when(crosser)
+    @pl.when(crosses)
     def _():
         for to in range(HEADS):
             cross_copy(to).wait_send()
 
     for half in range(2):
-        @pl.when(jnp.logical_not(last))
+        @pl.when(relays(half))
         def _():
-            for j in (0, 2, 4):
-                along(j, half).wait_send()
-
-        @pl.when(jnp.logical_not(last) & (core == 1))
-        def _():
-            ahead(half).wait_send()
-
-        @pl.when(core == 0)
-        def _():
-            beside(0, half).wait_send()
-        for j in (2, 4, 6):
-            beside(j, half).wait_send()
+            relay_copy(half).wait_send()
+
+    for half in range(2):
+        for j in (0, 2, 4, 6):
+            chain(j, half, lambda copy: copy.wait_send())
 
 
 def gather(q, k, v):
@@ -203,7 +236,9 @@
             pltpu.VMEM((2, ROWS * HEADS, WIDTH), jnp.float32),
             pltpu.VMEM((2, HEADS, ROWS, WIDTH), jnp.bfloat16),
             dma((4,)), dma((4,)), dma(()), dma((4,)), dma((4,)), dma(()), dma(()), dma((3, 2)), dma((4, 2)), dma((2,)),
-            dma((8, 2)), dma((4,)),
+            dma((8, 2)), dma((4,)), dma((2,)), dma((2,)),
+            pltpu.VMEM((2, 2, HALF, WIDTH), jnp.bfloat16),
+            pltpu.SemaphoreType.REGULAR,
         ],
         compiler_params=pltpu.CompilerParams(collective_id=0, has_side_effects=True),
         name="gather",

time: 69.1 us -> 57.9 us (0.84)
  the two profiles are of different devices: /device:TPU:33 before, /device:TPU:17 now
where the time goes in v2:
time: 57.9 us; the launch traced here: 57.3 us
  Pallas kernels  56.7 us (98%)
  between operations  0.64 us (1%)
    pallas_call x1, Pallas kernels, gather(): pl.pallas_call(gather_kernel, out_shape=(jax.ShapeDtypeStruct((HEADS, ROW...  47.5 us
    pallas_call x1, Pallas kernels, attend(): pl.pallas_call(attend_kernel, grid=(rows // CHUNK,), out_shape=(jax.Shape...  9.19 us

profile of v2, /device:TPU:17, one launch (start us, length us, event | category | flops | bytes accessed | tf_op | source)
XLA Modules:
  0.0 57.3 jit_solution(78441416145313894)
XLA Ops:
  0.6 47.5 %gather.1 = (bf16[4,64,8,128]{3,2,1,0:T(8,128)(2,1)}, bf16[2,2,8,128,128]{4,3,2,1,0:T(8,128)(2,1)}) custom-call(bf16[64,4,8,128]{3,2,1,0:T(8,128)(2,1)} %bitcast.8, bf16[256,128]{1,0:T(8,128)(2,1)} %bitcast.9, bf16[256,128]{1,0:T(8,128)(2,1)} %bitcast.10), custom_call_target="tpu_custom_call" | custom-call | tf_op jit(solution)/shard_map/gather/pallas_call | solution.py:227
  48.1 9.2 %attend.1 = (f32[2048,128]{1,0:T(8,128)}, f32[8,1,256]{2,1,0:T(1,128)}, f32[8,1,256]{2,1,0:T(1,128)}) custom-call(bf16[2048,128]{1,0:T(8,128)(2,1)} %bitcast.7, bf16[2,16,128,128]{3,2,1,0:T(8,128)(2,1)} %bitcast.6), custom_call_target="tpu_custom_call" | custom-call | tf_op jit(solution)/shard_map/attend/pallas_call | solution.py:323

commit v3 on v2

--- a/solution.py
+++ b/solution.py
@@ -21,7 +21,7 @@
 
 def gather_kernel(q_ref, k_ref, v_ref, q_out, x_out, wide, stage,
                   q_send, q_recv, q_own, s_send, s_recv, s_own, e_send, c_send, b_send, d_send, x_recv, w_send,
-                  r_recv, r_send, relay, ready):
+                  r_recv, r_send, relay, ready, go):
     c = lax.axis_index("ctx")
     h = lax.axis_index("head")
     core = lax.rem(c, 2)
@@ -38,10 +38,10 @@
     sibling = c + 1 - 2 * core
 
     def both(j):
-        return (over & (c - j >= BLOCK - 3)) | (c < 4)
+        return (over & (c - j >= BLOCK - 3)) | ((c < 2) & (j > c)) | ((c < 4) & (j >= c + 3))
 
     def both_next(j):
-        return (over & (c - j >= BLOCK - 3)) | (c < 2)
+        return (over & (c - j >= BLOCK - 3)) | ((c < 2) & (j >= c + 3))
 
     def wrapped(pair):
         return lax.rem(pair + PAIRS, PAIRS)
@@ -65,9 +65,12 @@
 
     @pl.when(crosser)
     def _():
-        for r in range(HEADS):
-            greet(across, r)
         greet(base + x_core, h)
+
+        @pl.when(jnp.logical_not(over))
+        def _():
+            for r in range(HEADS):
+                greet(across, r)
 
     for n, ref in enumerate((k_ref, v_ref)):
         wide[n] = ref[...].astype(jnp.float32)
@@ -77,8 +80,13 @@
 
     one, none = jnp.int32(1), jnp.int32(0)
     targets = (4 + lax.select(last, none, one) + lax.select(last | (core == 0), none, one)
-               + lax.select(crosser, one, none) * 4 + lax.select(near, one, none) * (4 - core))
+               + lax.select(crosser & over, one, none) * 4 + lax.select(near, one, none) * (4 - core))
     pl.semaphore_wait(bar, targets)
+
+    @pl.when(crosser & over)
+    def _():
+        for r in range(HEADS):
+            pl.semaphore_signal(go.at[h], inc=1, device_id=(across, r), device_id_type=MESH)
 
     @pl.when(near)
     def _():
@@ -115,7 +123,7 @@
 
     crosses = crosser & (over | (back <= 3) | (h < 2))
 
-    @pl.when(crosses)
+    @pl.when(crosses & over)
     def _():
         for to in range(HEADS):
             cross_copy(to).start()
@@ -184,11 +192,20 @@
                 arrive(2 * half + 1)
             chain(j, half, lambda copy: copy.start())
         if j == 0:
+            @pl.when(crosser & jnp.logical_not(over))
+            def _():
+                for to in range(HEADS):
+                    pl.semaphore_wait(go.at[to], 1)
+
+                    @pl.when(crosses)
+                    def _():
+                        cross_copy(to).start()
+
             @pl.when(crosser)
             def _():
                 pl.semaphore_wait(ready, 1)
 
-            for half in range(2):
+            for half in (1, 0):
                 @pl.when(relays(half))
                 def _():
                     remote(relay.at[:, half], relay.at[:, half], e_send, r_recv.at[half], c, h).wait_recv()
@@ -239,14 +256,16 @@
             dma((8, 2)), dma((4,)), dma((2,)), dma((2,)),
             pltpu.VMEM((2, 2, HALF, WIDTH), jnp.bfloat16),
             pltpu.SemaphoreType.REGULAR,
+            pltpu.SemaphoreType.REGULAR((HEADS,)),
         ],
         compiler_params=pltpu.CompilerParams(collective_id=0, has_side_effects=True),
         name="gather",
     )(q, k, v)
 
 
-CHUNK = 256
+CHUNK = 512
 TOKENS = CHUNK // GROUP
+PIECE = 4
 SCALE = 1.0 / math.sqrt(WIDTH)
 LOG2E = math.log2(math.e)
 LOW = -1e30
@@ -284,7 +303,8 @@
             stats[n, half] += jnp.sum(jnp.where(hit, wide, 0.0), axis=0)
 
     def whole(diagonal, *ranges):
-        pieces = [(diagonal, diagonal + 1), *(r for r in ranges if r[1] > r[0])]
+        cut = [(x, min(x + PIECE, b)) for a, b in ranges for x in range(a, b, PIECE)]
+        pieces = [(diagonal, diagonal + 1), *cut]
         s = []
         for n, (a, b) in enumerate(pieces):
             one = nt_dot(q, x_ref[0, a:b].reshape(-1, WIDTH))

time: 57.9 us -> 55.8 us (0.964)
  Pallas kernels: 56.7 us -> 54.9 us
    pallas_call x1, Pallas kernels: 9.19 us -> 6.7 us  [attend(): pl.pallas_call(attend_kernel, grid=(rows // CHUNK,), out_shape=(jax.Shape...]
    pallas_call x1, Pallas kernels: 47.5 us -> 48.2 us  [gather(): pl.pallas_call(gather_kernel, out_shape=(jax.ShapeDtypeStruct((HEADS, ROW...]
where the time goes in v3:
time: 55.8 us; the launch traced here: 55.6 us
  Pallas kernels  54.9 us (98%)
  between operations  0.64 us (1%)
    pallas_call x1, Pallas kernels, gather(): pl.pallas_call(gather_kernel, out_shape=(jax.ShapeDtypeStruct((HEADS, ROW...  48.2 us
    pallas_call x1, Pallas kernels, attend(): pl.pallas_call(attend_kernel, grid=(rows // CHUNK,), out_shape=(jax.Shape...  6.7 us

profile of v3, /device:TPU:17, one launch (start us, length us, event | category | flops | bytes accessed | tf_op | source)
XLA Modules:
  0.0 55.6 jit_solution(9685290659340891106)
XLA Ops:
  0.6 48.2 %gather.1 = (bf16[4,64,8,128]{3,2,1,0:T(8,128)(2,1)}, bf16[2,2,8,128,128]{4,3,2,1,0:T(8,128)(2,1)}) custom-call(bf16[64,4,8,128]{3,2,1,0:T(8,128)(2,1)} %bitcast.8, bf16[256,128]{1,0:T(8,128)(2,1)} %bitcast.9, bf16[256,128]{1,0:T(8,128)(2,1)} %bitcast.10), custom_call_target="tpu_custom_call" | custom-call | tf_op jit(solution)/shard_map/gather/pallas_call | solution.py:244
  48.9 6.7 %attend.1 = (f32[2048,128]{1,0:T(8,128)}, f32[8,1,256]{2,1,0:T(1,128)}, f32[8,1,256]{2,1,0:T(1,128)}) custom-call(bf16[2048,128]{1,0:T(8,128)(2,1)} %bitcast.7, bf16[2,16,128,128]{3,2,1,0:T(8,128)(2,1)} %bitcast.6), custom_call_target="tpu_custom_call" | custom-call | tf_op jit(solution)/shard_map/attend/pallas_call | solution.py:343

commit v4 on v3

--- a/solution.py
+++ b/solution.py
@@ -247,7 +247,7 @@
             jax.ShapeDtypeStruct((HEADS, ROWS, GROUP, WIDTH), jnp.bfloat16),
             jax.ShapeDtypeStruct((2, 2, WIN, HALF, WIDTH), jnp.bfloat16),
         ),
-        in_specs=[any_space, vmem, vmem],
+        in_specs=[pl.BlockSpec(memory_space=pltpu.HBM), vmem, vmem],
         out_specs=(any_space, any_space),
         scratch_shapes=[
             pltpu.VMEM((2, ROWS * HEADS, WIDTH), jnp.float32),
@@ -258,7 +258,7 @@
             pltpu.SemaphoreType.REGULAR,
             pltpu.SemaphoreType.REGULAR((HEADS,)),
         ],
-        compiler_params=pltpu.CompilerParams(collective_id=0, has_side_effects=True),
+        compiler_params=pltpu.CompilerParams(collective_id=0, has_side_effects=True, vmem_limit_bytes=8 << 20),
         name="gather",
     )(q, k, v)
 
@@ -360,6 +360,7 @@
         scratch_shapes=[
             pltpu.VMEM((2, 2, GROUP, HALF), jnp.float32),
         ],
+        compiler_params=pltpu.CompilerParams(vmem_limit_bytes=48 << 20),
         name="attend",
     )(q, x)
 

time: 55.8 us -> 56.9 us (1.020)
  the two profiles are of different devices: /device:TPU:17 before, /device:TPU:33 now
where the time goes in v4:
time: 56.9 us; the launch traced here: 56.6 us
  Pallas kernels  53.3 us (94%)
  local copies, waits for them, and re-layouts  2.71 us (5%)
  between operations  0.65 us (1%)
    pallas_call x1, Pallas kernels, gather(): pl.pallas_call(gather_kernel, out_shape=(jax.ShapeDtypeStruct((HEADS, ROW...  47.7 us
    pallas_call x1, Pallas kernels, attend(): pl.pallas_call(attend_kernel, grid=(rows // CHUNK,), out_shape=(jax.Shape...  5.59 us
    unnamed x6, local copies, waits for them, and re-layouts  2.71 us

profile of v4, /device:TPU:33, one launch (start us, length us, event | category | flops | bytes accessed | tf_op | source)
XLA Modules:
  0.0 56.6 jit_solution(13159388161979390599)
XLA Ops:
  0.6 0.0 copy-start
  0.6 1.0 %copy-done = bf16[1,64,32,128]{3,2,1,0:T(8,128)(2,1)S(1)} copy-done((bf16[1,64,32,128]{3,2,1,0:T(8,128)(2,1)S(1)}, bf16[1,64,32,128]{3,2,1,0:T(8,128)(2,1)}, u32[]{:S(2)}) %copy-start) | copy-done | bytes 524312
  1.7 0.0 copy-start.1
  1.7 0.8 %copy-done.1 = bf16[1,64,4,128]{3,2,1,0:T(4,128)(2,1)S(1)} copy-done((bf16[1,64,4,128]{3,2,1,0:T(4,128)(2,1)S(1)}, bf16[1,64,4,128]{3,2,1,0:T(4,128)(2,1)}, u32[]{:S(2)}) %copy-start.1) | copy-done | bytes 65560
  2.5 0.0 copy-start.2
  2.5 0.8 %copy-done.2 = bf16[1,64,4,128]{3,2,1,0:T(4,128)(2,1)S(1)} copy-done((bf16[1,64,4,128]{3,2,1,0:T(4,128)(2,1)S(1)}, bf16[1,64,4,128]{3,2,1,0:T(4,128)(2,1)}, u32[]{:S(2)}) %copy-start.2) | copy-done | bytes 65560
  3.4 47.7 %gather.1 = (bf16[4,64,8,128]{3,2,1,0:T(8,128)(2,1)S(1)}, bf16[2,2,8,128,128]{4,3,2,1,0:T(8,128)(2,1)S(1)}) custom-call(bf16[64,4,8,128]{3,2,1,0:T(8,128)(2,1)S(1)} %bitcast.8, bf16[256,128]{1,0:T(8,128)(2,1)S(1)} %bitcast.9, bf16[256,128]{1,0:T(8,128)(2,1)S(1)} %bitcast.10), custom_call_target="tpu_custom_call" | custom-call | tf_op jit(solution)/shard_map/gather/pallas_call | solution.py:244
  51.0 5.6 %attend.1 = (f32[2048,128]{1,0:T(8,128)}, f32[8,1,256]{2,1,0:T(1,128)}, f32[8,1,256]{2,1,0:T(1,128)}) custom-call(bf16[2048,128]{1,0:T(8,128)(2,1)S(1)} %bitcast.7, bf16[2,16,128,128]{3,2,1,0:T(8,128)(2,1)S(1)} %bitcast.6), custom_call_target="tpu_custom_call" | custom-call | tf_op jit(solution)/shard_map/attend/pallas_call | solution.py:343
Async XLA Ops:
  0.6 1.0 %copy-start = (bf16[1,64,32,128]{3,2,1,0:T(8,128)(2,1)S(1)}, bf16[1,64,32,128]{3,2,1,0:T(8,128)(2,1)}, u32[]{:S(2)}) copy-start(bf16[1,64,32,128]{3,2,1,0:T(8,128)(2,1)} %param.3) | copy-start | bytes 1572868
  1.7 0.8 %copy-start.1 = (bf16[1,64,4,128]{3,2,1,0:T(4,128)(2,1)S(1)}, bf16[1,64,4,128]{3,2,1,0:T(4,128)(2,1)}, u32[]{:S(2)}) copy-start(bf16[1,64,4,128]{3,2,1,0:T(4,128)(2,1)} %param.4) | copy-start | bytes 196612
  2.5 0.8 %copy-start.2 = (bf16[1,64,4,128]{3,2,1,0:T(4,128)(2,1)S(1)}, bf16[1,64,4,128]{3,2,1,0:T(4,128)(2,1)}, u32[]{:S(2)}) copy-start(bf16[1,64,4,128]{3,2,1,0:T(4,128)(2,1)} %param.5) | copy-start | bytes 196612
